TPU v7x, 32 devices: a whole 2x2x4 slice. The times are simulated.
32 devices in a mesh: dp: 4 (over y, core), fsdp: 4 (over z), tensor: 2 (over x).
Axes of the slice: x: 2, y: 2, z: 4, core: 2. Of those that a mesh axis runs over, the one named last changes fastest.
Arguments:
- hidden_in: bfloat16 [7168, 8192], P(('dp', 'fsdp')), may hold values from -6 to 6
- queries: bfloat16 [7168, 8192], P(('dp', 'fsdp'), 'tensor')
- keys: bfloat16 [7168, 1024], P(('dp', 'fsdp'), 'tensor')
- output_gradient: bfloat16 [7168, 8192], P(('dp', 'fsdp'), 'tensor'), may hold values from -6 to 6
- rewards: float32 [16], P(('dp', 'fsdp')), may hold values from 0 to 4
- lengths: int32 [16], P(('dp', 'fsdp')), may hold values from 112 to 448
- master: float32 [8192, 1024], P(('dp', 'fsdp'), 'tensor'), may hold values from -0.0625 to 0.0625
- moment: float32 [8192, 1024], P(('dp', 'fsdp'), 'tensor'), may hold values from -6 to 6
- adam_second_moment: float32 [8192, 1024], P(('dp', 'fsdp'), 'tensor'), may hold values from 0.25 to 4
- layout: int32 [8], replicated, may hold values from 0 to 7, each once
Outputs:
- updated_master_weight: float32 [8192, 1024], P(('dp', 'fsdp'), 'tensor')
- new_moment: float32 [8192, 1024], P(('dp', 'fsdp'), 'tensor')
- new_second: float32 [8192, 1024], P(('dp', 'fsdp'), 'tensor')
- rollout_value_weight: bfloat16 [8192, 1024], P(('dp', 'fsdp'), 'tensor')
All inputs are finite; a program needn't handle non-finite values.
Results may differ from a plain program's by a relative error of at most 0.0014.
Values may be sent and summed in bfloat16 or wider, within the bound.
A program may use at most 192 MiB of HBM per device.

v0:
```python
import jax
import jax.numpy as jnp
from jax import lax
from jax.sharding import PartitionSpec as P

HEAD_SIZE = 128
QUERY_PER_VALUE = 8


def value_grad(query_matrix, key_matrix, out_rows, value_weight, length):
    token_slot_index = query_matrix.shape[0]
    heads_local = key_matrix.shape[1] // HEAD_SIZE
    query_head_rows = query_matrix.reshape(
        token_slot_index, heads_local, QUERY_PER_VALUE, HEAD_SIZE
    )
    key_head_rows = key_matrix.reshape(token_slot_index, heads_local, HEAD_SIZE)
    scores = jnp.einsum(
        "tkgd,skd->kgts", query_head_rows, key_head_rows, preferred_element_type=jnp.float32
    ) / jnp.sqrt(jnp.float32(HEAD_SIZE))
    position = jnp.arange(token_slot_index)
    allowed = (position[None, :] <= position[:, None]) & (position[None, :] < length)
    scores = jnp.where(allowed[None, None], scores, jnp.float32(-1e30))
    top = jnp.max(scores, axis=-1, keepdims=True)
    expo = jnp.exp(scores - top)
    probs = (expo / jnp.sum(expo, axis=-1, keepdims=True)).astype(jnp.bfloat16)
    attention_gradient = (value_weight[:, None] * out_rows.astype(jnp.float32)).astype(jnp.bfloat16)
    head_gradient = attention_gradient.reshape(
        token_slot_index, heads_local, QUERY_PER_VALUE, HEAD_SIZE
    )
    value_gradient = jnp.einsum(
        "kgts,tkgd->skd", probs, head_gradient, preferred_element_type=jnp.float32
    )
    return value_gradient.reshape(token_slot_index, heads_local * HEAD_SIZE).astype(jnp.bfloat16)


def on_device(
    hidden_in,
    queries,
    keys,
    output_gradient,
    rewards,
    lengths,
    master,
    moment,
    adam_second_moment,
    layout,
):
    reward_sum, length_sum = lax.psum(
        (jnp.sum(rewards), jnp.sum(lengths).astype(jnp.float32)), ("dp", "fsdp")
    )
    seq_count = jnp.float32(lax.axis_size(("dp", "fsdp")))
    advantage = rewards[0] - reward_sum / seq_count
    position = jnp.arange(hidden_in.shape[0])
    value_weight = jnp.where(
        position < lengths[0], advantage * seq_count / length_sum, jnp.float32(0.0)
    )
    value_gradient = value_grad(queries, keys, output_gradient, value_weight, lengths[0])
    grad = lax.psum_scatter(
        lax.dot_general(
            hidden_in, value_gradient, (((0,), (0,)), ((), ())), preferred_element_type=jnp.float32
        ),
        ("dp", "fsdp"),
        scatter_dimension=0,
        tiled=True,
    )
    new_moment = 0.9 * moment + 0.1 * grad
    new_second = 0.95 * adam_second_moment + 0.05 * grad * grad
    corrected = new_moment / (1.0 - 0.9**10) / (jnp.sqrt(new_second / (1.0 - 0.95**10)) + 1e-08)
    updated_master_weight = master - 0.002 * (corrected + 0.1 * master)
    rounded_weight = updated_master_weight.astype(jnp.bfloat16)
    row_count = rounded_weight.shape[0]
    heads_local = rounded_weight.shape[1] // HEAD_SIZE
    targets = lax.dynamic_slice_in_dim(layout, lax.axis_index("tensor") * heads_local, heads_local)
    piece = lax.all_gather(rounded_weight, "tensor", axis=1, tiled=True)
    piece_heads = piece.shape[1] // HEAD_SIZE
    piece_rows = piece.reshape(row_count, piece_heads, HEAD_SIZE)
    carry_rows = jnp.zeros_like(rounded_weight).reshape(row_count, heads_local, HEAD_SIZE)
    chosen = []
    for slot in range(heads_local):
        wanted = targets[slot]
        inside = (wanted >= 0) & (wanted < piece_heads)
        offset = jnp.clip(wanted, 0, piece_heads - 1)
        candidate = lax.dynamic_index_in_dim(piece_rows, offset, 1, keepdims=False)
        chosen.append(jnp.where(inside, candidate, carry_rows[:, slot]))
    rollout_value_weight = jnp.stack(chosen, axis=1).reshape(row_count, heads_local * HEAD_SIZE)
    return (updated_master_weight, new_moment, new_second, rollout_value_weight)


def solution(mesh):
    placed = (
        P(("dp", "fsdp"), None),
        P(("dp", "fsdp"), "tensor"),
        P(("dp", "fsdp"), "tensor"),
        P(("dp", "fsdp"), "tensor"),
        P(("dp", "fsdp")),
        P(("dp", "fsdp")),
        P(("dp", "fsdp"), "tensor"),
        P(("dp", "fsdp"), "tensor"),
        P(("dp", "fsdp"), "tensor"),
        P(),
    )
    return jax.shard_map(
        on_device,
        mesh=mesh,
        in_specs=placed,
        out_specs=(
            P(("dp", "fsdp"), "tensor"),
            P(("dp", "fsdp"), "tensor"),
            P(("dp", "fsdp"), "tensor"),
            P(("dp", "fsdp"), "tensor"),
        ),
        check_vma=False,
    )
```

profile of v0, /device:TPU:0, one launch (start us, length us, event | category | flops | bytes accessed | tf_op | source)
XLA Modules:
  0.0 377.8 jit_solution(9101465570995655895)
XLA Ops:
  7.2 0.0 reduce-scatter.2.cloned.1.call-start
  8.6 35.8 %all-reduce = (f32[]{:T(128)}, f32[]{:T(128)}) all-reduce(f32[]{:T(128)} %bitcast.1, f32[]{:T(128)S(6)} %convert_element_type.24), channel_id=1, replica_groups=mesh['dp'=4,'fsdp'=4,'tensor'=2] {'dp','fsdp'}, use_global_device_ids=true, to_apply=%region_0.0 | all-reduce | flops 2 | bytes 16 | tf_op jit(solution)/shard_map/psum | solution.py:48
  45.7 0.0 copy-start
  45.7 3.3 fusion.5
  49.1 2.8 copy.44
  51.9 0.1 fusion.11
  52.0 2.9 copy.45
  54.9 0.1 reshape.103
  55.0 16.2 %fusion.6 = f32[4,448,448,8]{2,1,3,0:T(8,128)} fusion(bf16[448,4,8,128]{3,2,1,0:T(8,128)(2,1)} %bitcast.53, bf16[448,4,128,1]{2,1,0,3:T(4,128)(2,1)S(1)} %bitcast.56), kind=kOutput, calls=%fused_computation.11 | convolution fusion | flops 1644167168 | bytes 29818880 | tf_op jit(solution)/shard_map/tkgd,skd->kgts/dot_general | solution.py:17
  71.3 29.3 %fusion.20 = (f32[4,8,448]{2,1,0:T(8,128)S(1)}, f32[4,8,448,448]{2,3,1,0:T(8,128)}) fusion(f32[4,448,448,8]{2,1,3,0:T(8,128)} %fusion.6, pred[448,448]{0,1:T(8,128)(4,1)S(1)} %fusion.11), kind=kOutput, calls=%fused_computation.36 | output fusion | flops 38535616 | bytes 51638272 | tf_op jit(solution)/shard_map/sub | solution.py:24
  100.6 17.7 %divide_convert_fusion = bf16[4,8,448,448]{2,3,1,0:T(8,128)(2,1)} fusion(f32[4,8,448,448]{2,3,1,0:T(8,128)} %get-tuple-element.27, f32[4,8,448]{2,1,0:T(8,128)S(1)} %get-tuple-element.26), kind=kLoop, calls=%fused_computation.2 | loop fusion | flops 12845056 | bytes 38592512 | tf_op jit(solution)/shard_map/convert_element_type | solution.py:25
  118.2 28.1 %copy.39 = bf16[4,8,448,448]{3,1,0,2:T(8,128)(2,1)} copy(bf16[4,8,448,448]{2,3,1,0:T(8,128)(2,1)} %divide_convert_fusion) | data formatting | bytes 25690112 | tf_op jit(solution)/shard_map/convert_element_type | solution.py:25
  146.3 11.0 %fusion.9 = bf16[4,56,8,128]{3,2,1,0:T(8,128)(2,1)S(1)} fusion(bf16[448,4,8,128]{3,2,1,0:T(8,128)(2,1)} %bitcast.52, bf16[4,8,448,448]{3,1,0,2:T(8,128)(2,1)} %copy.39), kind=kOutput, calls=%fused_computation.16 | convolution fusion | flops 1644396544 | bytes 16973824 | tf_op jit(solution)/shard_map/kgts,tkgd->skd/dot_general | solution.py:30
  157.2 11.2 %convolution_bitcast_fusion = f32[8192,512]{0,1:T(8,128)} fusion(bf16[448,8192]{1,0:T(8,128)(2,1)} %param.10, bf16[4,56,8,128]{3,2,1,0:T(8,128)(2,1)S(1)} %fusion.9), kind=kOutput, calls=%fused_computation.8 | convolution fusion | flops 3758096384 | bytes 24576000 | tf_op jit(solution)/shard_map/dot_general | solution.py:59
  168.5 0.0 reduce-scatter.2.cloned.1.call-update
  168.5 0.0 all-gather.2.cloned.1.call-start
  168.5 1.1 copy-done.1
  169.7 1.3 copy.25
  171.0 1.3 copy.30
  172.3 1.3 copy.32
  173.6 170.9 %reduce-scatter.2.cloned.1.call-done = f32[512,512]{0,1:T(8,128)} async-done(((f32[8192,512]{0,1:T(8,128)}), f32[512,512]{0,1:T(8,128)}) %reduce-scatter.2.cloned.1.call-update) | async-done | bytes 1048592 | tf_op jit(solution)/shard_map/reduce_scatter | solution.py:58
  344.5 3.8 %fusion.17 = (bf16[512,512]{0,1:T(8,128)(2,1)}, f32[512,512]{0,1:T(8,128)S(1)}, f32[512,512]{0,1:T(8,128)S(1)}, f32[512,512]{0,1:T(8,128)S(1)}) fusion(f32[512,512]{0,1:T(8,128)} %copy.32, f32[512,512]{0,1:T(8,128)} %reduce-scatter.2.cloned.1.call-done, f32[512,512]{0,1:T(8,128)} %copy.25, f32[512,512]{0,1:T(8,128)} %copy.30), kind=kLoop, calls=%fused_computation.34 | loop fusion | flops 4194304 | bytes 7864320 | tf_op jit(solution)/shard_map/convert_element_type | solution.py:70
  348.3 0.0 all-gather.2.cloned.1.call-update
  348.3 0.1 dynamic_slice.16
  348.4 0.7 fusion.19
  356.8 1.3 copy.34
  358.1 1.3 copy.35
  359.4 1.3 copy.36
  360.7 8.1 %all-gather.2.cloned.1.call-done = bf16[512,1024]{0,1:T(8,128)(2,1)} async-done(((bf16[512,512]{0,1:T(8,128)(2,1)}), bf16[512,1024]{0,1:T(8,128)(2,1)}) %all-gather.2.cloned.1.call-update) | async-done | bytes 1048592 | tf_op jit(solution)/shard_map/all_gather | solution.py:74
  368.8 1.1 dynamic-slice_select_fusion.3
  369.9 0.1 pad_maximum_fusion
  370.0 1.0 copy.42
  (12 shorter events, 0.0 us)
Async XLA Ops:
  7.2 47.7 %copy-start.4 = (bf16[448,512]{1,0:T(8,128)(2,1)S(1)}, bf16[448,512]{1,0:T(8,128)(2,1)}, u32[]{:S(2)}) copy-start(bf16[448,512]{1,0:T(8,128)(2,1)} %param.12) | copy-start | bytes 1376260
  7.2 337.3 %reduce-scatter.2.cloned.1.call-start = ((), (), s32[]{:S(2)}) async-start(), calls=%async_computation.1 | async-start | bytes 17825792 | tf_op jit(solution)/shard_map/reduce_scatter | solution.py:58
  45.7 6.3 %copy-start = (bf16[448,4096]{1,0:T(8,128)(2,1)S(1)}, bf16[448,4096]{1,0:T(8,128)(2,1)}, u32[]{:S(2)}) copy-start(bf16[448,4096]{1,0:T(8,128)(2,1)} %param.11) | copy-start | bytes 11010052
  168.4 1.2 copy-start.1
  168.4 2.5 copy-start.2
  168.5 3.8 %copy-start.3 = (f32[512,512]{1,0:T(8,128)S(1)}, f32[512,512]{1,0:T(8,128)}, u32[]{:S(2)}) copy-start(f32[512,512]{1,0:T(8,128)} %param.16) | copy-start | bytes 3145732
  168.5 179.9 %copy-start.5 = (s32[8]{0:T(128)S(1)}, s32[8]{0:T(128)}, u32[]{:S(2)}) copy-start(s32[8]{0:T(128)} %param.19) | copy-start | bytes 100
  168.5 200.3 %all-gather.2.cloned.1.call-start = ((), (), s32[]{:S(2)}) async-start(), calls=%async_computation.2 | async-start | bytes 1572864 | tf_op jit(solution)/shard_map/all_gather | solution.py:74
Sparse Core Ops, SparseCore 0:
  168.6 175.8 reduce-scatter.1
  348.4 20.2 all-gather.1
where the time goes:
time: 379 us; the launch traced here: 378 us
  waiting for transfers between devices  179 us (47%)
  other arithmetic  55.4 us (15%)
  local copies, waits for them, and re-layouts  44.6 us (12%)
  matrix products  38.4 us (10%)
  blocking collectives  35.8 us (9%)
  between operations  24.5 us (6%)
    reduce_scatter x1, waiting for transfers between devices, on_device(): lax.psum_scatter(lax.dot_general(hidden_in, value_gradient, (((0,), (0,))...  171 us
    psum x1, blocking collectives, on_device(): lax.psum((jnp.sum(rewards), jnp.sum(lengths).astype(jnp.float32)), ('dp',...  35.8 us
    sub x1, other arithmetic, value_grad(): expo = jnp.exp(scores - top)  29.3 us
    convert_element_type x1, local copies, waits for them, and re-layouts, value_grad(): probs = (expo / jnp.sum(expo, axis=-1, keepdims=True)).astype(jnp.bfloat16)  28.1 us
    convert_element_type x1, other arithmetic, value_grad(): probs = (expo / jnp.sum(expo, axis=-1, keepdims=True)).astype(jnp.bfloat16)  17.7 us
    dot_general x1, matrix products, value_grad(): jnp.einsum('tkgd,skd->kgts', query_head_rows, key_head_rows, preferred_el...  16.2 us
    unnamed x20, local copies, waits for them, and re-layouts  14.7 us
    dot_general x1, matrix products, on_device(): lax.dot_general(hidden_in, value_gradient, (((0,), (0,)), ((), ())), pref...  11.2 us
  transfers between devices with their start and end apart: 2, of which 2 were waited for; matrix products, arithmetic and copies ran while one was open for 2% of the time, Pallas kernels for 0%

commit v1 on v0

--- a/solution.py
+++ b/solution.py
@@ -46,7 +46,7 @@
     layout,
 ):
     reward_sum, length_sum = lax.psum(
-        (jnp.sum(rewards), jnp.sum(lengths).astype(jnp.float32)), ("dp", "fsdp")
+        lax.psum((jnp.sum(rewards), jnp.sum(lengths).astype(jnp.float32)), "fsdp"), "dp"
     )
     seq_count = jnp.float32(lax.axis_size(("dp", "fsdp")))
     advantage = rewards[0] - reward_sum / seq_count

time: 379 us -> 365 us (0.963)
  blocking collectives: 35.8 us -> 20.4 us
    psum x1 -> x2, blocking collectives: 35.8 us -> 20.4 us  [the longest x1 14.1 us: on_device(): lax.psum((jnp.sum(rewards), jnp.sum(lengths).astype(jnp.float32)), 'fsdp')]
where the time goes in v1:
time: 365 us; the launch traced here: 363 us
  waiting for transfers between devices  180 us (49%)
  other arithmetic  55.4 us (15%)
  local copies, waits for them, and re-layouts  44.5 us (12%)
  matrix products  38.4 us (11%)
  between operations  24.4 us (7%)
  blocking collectives  20.4 us (6%)
    reduce_scatter x1, waiting for transfers between devices, on_device(): lax.psum_scatter(lax.dot_general(hidden_in, value_gradient, (((0,), (0,))...  172 us
    sub x1, other arithmetic, value_grad(): expo = jnp.exp(scores - top)  29.3 us
    convert_element_type x1, local copies, waits for them, and re-layouts, value_grad(): probs = (expo / jnp.sum(expo, axis=-1, keepdims=True)).astype(jnp.bfloat16)  28 us
    convert_element_type x1, other arithmetic, value_grad(): probs = (expo / jnp.sum(expo, axis=-1, keepdims=True)).astype(jnp.bfloat16)  17.7 us
    dot_general x1, matrix products, value_grad(): jnp.einsum('tkgd,skd->kgts', query_head_rows, key_head_rows, preferred_el...  16.2 us
    unnamed x20, local copies, waits for them, and re-layouts  14.7 us
    psum x1, blocking collectives, on_device(): lax.psum((jnp.sum(rewards), jnp.sum(lengths).astype(jnp.float32)), 'fsdp')  14.1 us
    dot_general x1, matrix products, on_device(): lax.dot_general(hidden_in, value_gradient, (((0,), (0,)), ((), ())), pref...  11.2 us
  transfers between devices with their start and end apart: 2, of which 2 were waited for; matrix products, arithmetic and copies ran while one was open for 2% of the time, Pallas kernels for 0%

profile of v1, /device:TPU:0, one launch (start us, length us, event | category | flops | bytes accessed | tf_op | source)
XLA Modules:
  0.0 363.5 jit_solution(8970696082748298716)
XLA Ops:
  7.2 0.0 reduce-scatter.2.cloned.1.call-start
  8.6 14.1 %all-reduce = (f32[]{:T(128)}, f32[]{:T(128)}) all-reduce(f32[]{:T(128)} %bitcast.1, f32[]{:T(128)S(6)} %convert_element_type.24), channel_id=1, replica_groups=mesh['dp'=4,'fsdp'=4,'tensor'=2] {'fsdp'}, use_global_device_ids=true, to_apply=%region_0.0 | all-reduce | flops 2 | bytes 16 | tf_op jit(solution)/shard_map/psum | solution.py:49
  22.7 6.3 %all-reduce.1 = (f32[]{:T(128)}, f32[]{:T(128)}) all-reduce(f32[]{:T(128)} %get-tuple-element.12, f32[]{:T(128)} %get-tuple-element.13), channel_id=1, replica_groups=mesh['dp'=4,'fsdp'=4,'tensor'=2] {'dp'}, use_global_device_ids=true, to_apply=%region_1.0 | all-reduce | flops 2 | bytes 16 | tf_op jit(solution)/shard_map/psum | solution.py:48
  30.3 3.3 fusion.5
  33.6 2.8 copy.44
  36.5 0.1 fusion.11
  36.6 2.9 copy.45
  39.5 0.1 reshape.103
  39.6 16.2 %fusion.6 = f32[4,448,448,8]{2,1,3,0:T(8,128)} fusion(bf16[448,4,8,128]{3,2,1,0:T(8,128)(2,1)} %bitcast.53, bf16[448,4,128,1]{2,1,0,3:T(4,128)(2,1)S(1)} %bitcast.56), kind=kOutput, calls=%fused_computation.11 | convolution fusion | flops 1644167168 | bytes 29818880 | tf_op jit(solution)/shard_map/tkgd,skd->kgts/dot_general | solution.py:17
  55.8 29.3 %fusion.20 = (f32[4,8,448]{2,1,0:T(8,128)S(1)}, f32[4,8,448,448]{2,3,1,0:T(8,128)}) fusion(f32[4,448,448,8]{2,1,3,0:T(8,128)} %fusion.6, pred[448,448]{0,1:T(8,128)(4,1)S(1)} %fusion.11), kind=kOutput, calls=%fused_computation.36 | output fusion | flops 38535616 | bytes 51638272 | tf_op jit(solution)/shard_map/sub | solution.py:24
  85.1 17.7 %divide_convert_fusion = bf16[4,8,448,448]{2,3,1,0:T(8,128)(2,1)} fusion(f32[4,8,448,448]{2,3,1,0:T(8,128)} %get-tuple-element.29, f32[4,8,448]{2,1,0:T(8,128)S(1)} %get-tuple-element.28), kind=kLoop, calls=%fused_computation.2 | loop fusion | flops 12845056 | bytes 38592512 | tf_op jit(solution)/shard_map/convert_element_type | solution.py:25
  102.8 28.0 %copy.39 = bf16[4,8,448,448]{3,1,0,2:T(8,128)(2,1)} copy(bf16[4,8,448,448]{2,3,1,0:T(8,128)(2,1)} %divide_convert_fusion) | data formatting | bytes 25690112 | tf_op jit(solution)/shard_map/convert_element_type | solution.py:25
  130.8 11.0 %fusion.9 = bf16[4,56,8,128]{3,2,1,0:T(8,128)(2,1)S(1)} fusion(bf16[448,4,8,128]{3,2,1,0:T(8,128)(2,1)} %bitcast.52, bf16[4,8,448,448]{3,1,0,2:T(8,128)(2,1)} %copy.39), kind=kOutput, calls=%fused_computation.16 | convolution fusion | flops 1644396544 | bytes 16973824 | tf_op jit(solution)/shard_map/kgts,tkgd->skd/dot_general | solution.py:30
  141.8 11.2 %convolution_bitcast_fusion = f32[8192,512]{0,1:T(8,128)} fusion(bf16[448,8192]{1,0:T(8,128)(2,1)} %param.10, bf16[4,56,8,128]{3,2,1,0:T(8,128)(2,1)S(1)} %fusion.9), kind=kOutput, calls=%fused_computation.8 | convolution fusion | flops 3758096384 | bytes 24576000 | tf_op jit(solution)/shard_map/dot_general | solution.py:59
  153.0 0.0 reduce-scatter.2.cloned.1.call-update
  153.0 0.0 all-gather.2.cloned.1.call-start
  153.1 1.1 copy-done.1
  154.2 1.3 copy.25
  155.5 1.3 copy.30
  156.8 1.3 copy.32
  158.1 172.0 %reduce-scatter.2.cloned.1.call-done = f32[512,512]{0,1:T(8,128)} async-done(((f32[8192,512]{0,1:T(8,128)}), f32[512,512]{0,1:T(8,128)}) %reduce-scatter.2.cloned.1.call-update) | async-done | bytes 1048592 | tf_op jit(solution)/shard_map/reduce_scatter | solution.py:58
  330.1 3.8 %fusion.17 = (bf16[512,512]{0,1:T(8,128)(2,1)}, f32[512,512]{0,1:T(8,128)S(1)}, f32[512,512]{0,1:T(8,128)S(1)}, f32[512,512]{0,1:T(8,128)S(1)}) fusion(f32[512,512]{0,1:T(8,128)} %copy.32, f32[512,512]{0,1:T(8,128)} %reduce-scatter.2.cloned.1.call-done, f32[512,512]{0,1:T(8,128)} %copy.25, f32[512,512]{0,1:T(8,128)} %copy.30), kind=kLoop, calls=%fused_computation.34 | loop fusion | flops 4194304 | bytes 7864320 | tf_op jit(solution)/shard_map/convert_element_type | solution.py:70
  333.9 0.0 all-gather.2.cloned.1.call-update
  333.9 0.1 dynamic_slice.16
  334.0 0.6 fusion.19
  342.2 1.3 copy.34
  343.5 1.3 copy.35
  344.8 1.3 copy.36
  346.1 8.3 %all-gather.2.cloned.1.call-done = bf16[512,1024]{0,1:T(8,128)(2,1)} async-done(((bf16[512,512]{0,1:T(8,128)(2,1)}), bf16[512,1024]{0,1:T(8,128)(2,1)}) %all-gather.2.cloned.1.call-update) | async-done | bytes 1048592 | tf_op jit(solution)/shard_map/all_gather | solution.py:74
  354.4 1.1 dynamic-slice_select_fusion.3
  355.5 0.1 pad_maximum_fusion
  355.6 1.0 copy.42
  (13 shorter events, 0.0 us)
Async XLA Ops:
  7.2 32.3 %copy-start.4 = (bf16[448,512]{1,0:T(8,128)(2,1)S(1)}, bf16[448,512]{1,0:T(8,128)(2,1)}, u32[]{:S(2)}) copy-start(bf16[448,512]{1,0:T(8,128)(2,1)} %param.12) | copy-start | bytes 1376260
  7.2 322.9 %reduce-scatter.2.cloned.1.call-start = ((), (), s32[]{:S(2)}) async-start(), calls=%async_computation.1 | async-start | bytes 17825792 | tf_op jit(solution)/shard_map/reduce_scatter | solution.py:58
  30.3 6.3 %copy-start = (bf16[448,4096]{1,0:T(8,128)(2,1)S(1)}, bf16[448,4096]{1,0:T(8,128)(2,1)}, u32[]{:S(2)}) copy-start(bf16[448,4096]{1,0:T(8,128)(2,1)} %param.11) | copy-start | bytes 11010052
  153.0 1.2 copy-start.1
  153.0 2.5 copy-start.2
  153.0 3.8 %copy-start.3 = (f32[512,512]{1,0:T(8,128)S(1)}, f32[512,512]{1,0:T(8,128)}, u32[]{:S(2)}) copy-start(f32[512,512]{1,0:T(8,128)} %param.16) | copy-start | bytes 3145732
  153.0 180.9 %copy-start.5 = (s32[8]{0:T(128)S(1)}, s32[8]{0:T(128)}, u32[]{:S(2)}) copy-start(s32[8]{0:T(128)} %param.19) | copy-start | bytes 100
  153.0 201.4 %all-gather.2.cloned.1.call-start = ((), (), s32[]{:S(2)}) async-start(), calls=%async_computation.2 | async-start | bytes 1572864 | tf_op jit(solution)/shard_map/all_gather | solution.py:74
Sparse Core Ops, SparseCore 0:
  153.2 176.8 reduce-scatter.1
  334.0 20.3 all-gather.1
